TPU v7x, 128 devices: a whole 4x4x4 slice. The times are simulated.
128 devices in a mesh: row: 8 (over x, core), col: 16 (over y, z).
Axes of the slice: x: 4, y: 4, z: 4, core: 2. Of those that a mesh axis runs over, the one named last changes fastest.
Arguments:
- series: bfloat16 [512, 32768], P(None, ('row', 'col')), may hold values from -6 to 6
- lag_weight: float32 [4], replicated, may hold values from 0.25 to 1
- start_basis: bfloat16 [64, 32768], P(None, ('row', 'col')), may hold values from -5.25 to 5.25
- block_pairs: int32 [8, 16, 32, 2], P('row', 'col'), may hold values from 0 to 127, as said below
- pair_count: int32 [8, 16], P('row', 'col'), may hold values from 1 to 32, as said below
Outputs:
- basis: float32 [64, 32768], P(None, ('row', 'col'))
- rayleigh: float32 [64, 64], replicated
Inputs may be any that keep to these rules, and one draw needn't show every extreme that they name: For every slot s of device (r, c), block_pairs[r, c, s, 0] is a block of row group r, from r * 16 to (r + 1) * 16 - 1, and block_pairs[r, c, s, 1] is a block held by a device of mesh column c: (block_pairs[r, c, s, 1]) mod (16) equals c. Slots that are not live hold blocks of the same ranges and are no part of the network. `pair_count`: the number of live slots of device (r, c); some device has exactly 32.
All inputs are finite; a program needn't handle non-finite values.
Results may differ from a plain program's by a relative error of at most 0.0045.
Values may be sent and summed in bfloat16 or wider, within the bound.
No kernel may reach another device: no remote copies, remote signals or barrier semaphores. Data moves between devices by JAX's collectives and lax.ppermute only.
A program may use at most 64 MiB of HBM per device.

v0:
```python
import math
import jax
import jax.numpy as jnp
from jax import lax
from jax.sharding import PartitionSpec as P

BLOCK = 256
ITERS = 2
BETA_CORR = 8.0
GRAM_EPS = 1e-05
HIGHEST = lax.Precision.HIGHEST


def lagged_tile(lead_block, trail_block, lag_weight, tile_scale):
    day_count = lead_block.shape[0]
    block_width = lead_block.shape[1]
    lag_count = lag_weight.shape[0]
    zero_rows = jnp.zeros((lag_count, block_width), lead_block.dtype)
    lead_padded = jnp.concatenate([lead_block, zero_rows], axis=0)
    trail_padded = jnp.concatenate([trail_block, zero_rows], axis=0)
    lead_shifted = jnp.concatenate(
        [lead_padded[offset : offset + day_count] for offset in range(lag_count)], axis=1
    )
    trail_shifted = jnp.concatenate(
        [trail_padded[offset : offset + day_count] for offset in range(lag_count)], axis=1
    )
    contract = (((0,), (0,)), ((), ()))
    forward = lax.dot_general(
        lead_shifted, trail_block, contract, preferred_element_type=jnp.float32
    )
    backward = lax.dot_general(
        lead_block, trail_shifted, contract, preferred_element_type=jnp.float32
    )
    forward = forward.reshape(lag_count, block_width, block_width)
    backward = jnp.transpose(backward.reshape(block_width, lag_count, block_width), (1, 0, 2))
    soft_corr = jnp.tanh(BETA_CORR / day_count * (forward + backward))
    weighted = jnp.sum(lag_weight[:, None, None] * soft_corr, axis=0)
    return (tile_scale * weighted).astype(jnp.bfloat16)


def local(series, lag_weight, start_basis, block_pairs, pair_count):
    n_rows = lax.axis_size("row")
    n_cols = lax.axis_size("col")
    row_index = lax.axis_index("row")
    local_cells = series.shape[1]
    local_blocks = local_cells // BLOCK
    row_blocks = local_blocks * n_cols
    col_blocks = local_blocks * n_rows
    slot_total = block_pairs.shape[2]
    cell_total = local_cells * n_rows * n_cols
    rank_size = start_basis.shape[0]
    tile_scale = 0.25 / math.sqrt(BLOCK)
    row_series = lax.all_gather(series, "col", axis=1, tiled=True)
    col_series = lax.all_gather(series, "row", axis=1, tiled=True)
    slot_pairs = block_pairs.reshape(slot_total, 2)
    slot_count = pair_count.reshape(1)
    row_first = row_index * row_blocks
    slot_ids = jnp.arange(slot_total, dtype=jnp.int32)
    own_rows = slot_pairs[:, 0] - row_first
    global_block = slot_pairs[:, 1]
    own_cols = global_block // local_blocks // n_cols * local_blocks + global_block % local_blocks
    built_count = slot_count[0]
    tile_rows = own_rows
    tile_cols = own_cols
    tile_rows = jnp.clip(tile_rows, 0, row_blocks - 1)
    tile_cols = jnp.clip(tile_cols, 0, col_blocks - 1)
    live_slots = slot_ids < built_count

    def build_one(slot, tiles):
        lead_block = lax.dynamic_slice_in_dim(row_series, tile_rows[slot] * BLOCK, BLOCK, 1)
        trail_block = lax.dynamic_slice_in_dim(col_series, tile_cols[slot] * BLOCK, BLOCK, 1)
        tile = lagged_tile(lead_block, trail_block, lag_weight, tile_scale)
        return lax.dynamic_update_index_in_dim(tiles, tile, slot, 0)

    tiles = lax.fori_loop(
        0, built_count, build_one, jnp.zeros((slot_total, BLOCK, BLOCK), jnp.bfloat16)
    )
    live_float = live_slots.astype(jnp.float32)[:, None]
    row_onehot = (tile_rows[:, None] == jnp.arange(row_blocks, dtype=jnp.int32)[None, :]).astype(
        jnp.float32
    ) * live_float
    col_onehot = (tile_cols[:, None] == jnp.arange(col_blocks, dtype=jnp.int32)[None, :]).astype(
        jnp.float32
    ) * live_float

    def project(basis_now):
        row_basis = lax.all_gather(basis_now, "col", axis=1, tiled=True).reshape(
            rank_size, row_blocks, BLOCK
        )
        col_basis = lax.all_gather(basis_now, "row", axis=1, tiled=True)
        col_basis = col_basis.reshape(rank_size, col_blocks, BLOCK)
        lead_basis = jnp.take(row_basis, tile_rows, axis=1)
        trail_basis = jnp.take(col_basis, tile_cols, axis=1)
        into_cols = jnp.einsum(
            "ksa,sab->ksb", lead_basis, tiles, preferred_element_type=jnp.float32
        )
        return (trail_basis, into_cols)

    def network_product(basis_now):
        trail_basis, into_cols = project(basis_now)
        into_rows = jnp.einsum(
            "ksb,sab->ksa", trail_basis, tiles, preferred_element_type=jnp.float32
        )
        row_part = jnp.einsum("ksa,sr->kra", into_rows, row_onehot, precision=HIGHEST)
        row_part = row_part.reshape(rank_size, row_blocks * BLOCK)
        col_part = jnp.einsum("ksb,sr->krb", into_cols, col_onehot, precision=HIGHEST)
        col_part = col_part.reshape(rank_size, col_blocks * BLOCK)
        row_total = lax.psum_scatter(row_part, "col", scatter_dimension=1, tiled=True)
        col_total = lax.psum_scatter(col_part, "row", scatter_dimension=1, tiled=True)
        return row_total + col_total

    current = start_basis
    basis = start_basis.astype(jnp.float32)
    for iteration in range(ITERS):
        product = network_product(current)
        local_gram = jnp.dot(product, product.T, precision=HIGHEST)
        gram = lax.psum(local_gram, ("row", "col")) / cell_total
        gram = gram + GRAM_EPS * jnp.eye(rank_size, dtype=jnp.float32)
        lower = jnp.linalg.cholesky(gram)
        basis = lax.linalg.triangular_solve(lower, product, left_side=True, lower=True)
        current = basis.astype(jnp.bfloat16)
    final = network_product(current)
    local_form = jnp.dot(final, current.astype(jnp.float32).T, precision=HIGHEST)
    rayleigh = lax.psum(local_form, ("row", "col")) / cell_total
    return (basis, rayleigh)


def solution(mesh):
    return jax.shard_map(
        local,
        mesh=mesh,
        in_specs=(
            P(None, ("row", "col")),
            P(),
            P(None, ("row", "col")),
            P("row", "col", None, None),
            P("row", "col"),
        ),
        out_specs=(P(None, ("row", "col")), P()),
        check_vma=False,
    )
```

profile of v0, /device:TPU:1, one launch (start us, length us, event | category | flops | bytes accessed | tf_op | source)
XLA Modules:
  0.0 914.3 jit_solution(11842656236986724844)
XLA Ops:
  8.0 0.7 all-gather.3.cloned.1.call-update
  8.7 14.7 %all_gather.26 = bf16[64,2048]{1,0:T(8,128)(2,1)S(1)} all-gather(bf16[64,256]{1,0:T(8,128)(2,1)} %param.16), channel_id=1, replica_groups=mesh['row'=8,'col'=16] {'row'}, dimensions={1}, use_global_device_ids=true | all-gather | bytes 294912 | tf_op jit(solution)/shard_map/all_gather | solution.py:90
  24.1 22.2 %all_gather.27 = bf16[64,4096]{1,0:T(8,128)(2,1)S(1)} all-gather(bf16[64,256]{1,0:T(8,128)(2,1)} %param.16), channel_id=1, replica_groups=mesh['row'=8,'col'=16] {'col'}, dimensions={1}, use_global_device_ids=true | all-gather | bytes 557056 | tf_op jit(solution)/shard_map/all_gather | solution.py:87
  47.1 51.3 %all-gather.3.cloned.1.call-done = bf16[512,4096]{1,0:T(8,128)(2,1)} async-done(((bf16[512,256]{1,0:T(8,128)(2,1)}), bf16[512,4096]{1,0:T(8,128)(2,1)}) %all-gather.3.cloned.1.call-update) | async-done | bytes 4194320 | tf_op jit(solution)/shard_map/all_gather | solution.py:53
  98.4 2.4 broadcast_in_dim.30
  100.8 116.0 %while.10 = (s32[]{:T(128)}, bf16[32,256,256]{2,1,0:T(8,128)(2,1)}, s32[]{:T(128)}, f32[4]{0:T(128)S(1)}, s32[32]{0:T(128)S(1)}, /*index=5*/bf16[512,4096]{1,0:T...) while((s32[]{:T(128)}, bf16[32,256,256]{2,1,0:T(8,128)(2,1)}, ...), condition=%wide.region_2.3_spmd, body=%wide.region_0.2_spmd.sunk | while | flops 546373632 | bytes 10617143 | solution.py:75
  104.0 1.1 constant_dynamic-slice_fusion.3
  110.4 1.1 constant_dynamic-slice_fusion.3
  116.8 1.1 constant_dynamic-slice_fusion.3
  123.2 1.1 constant_dynamic-slice_fusion.3
  129.6 1.1 constant_dynamic-slice_fusion.3
  136.0 1.1 constant_dynamic-slice_fusion.3
  142.4 1.1 constant_dynamic-slice_fusion.3
  148.8 1.1 constant_dynamic-slice_fusion.3
  155.2 1.1 constant_dynamic-slice_fusion.3
  161.6 1.1 constant_dynamic-slice_fusion.3
  168.0 1.1 constant_dynamic-slice_fusion.3
  174.4 1.1 constant_dynamic-slice_fusion.3
  180.9 1.1 constant_dynamic-slice_fusion.3
  187.3 1.1 constant_dynamic-slice_fusion.3
  193.7 1.1 constant_dynamic-slice_fusion.3
  200.1 1.1 constant_dynamic-slice_fusion.3
  206.5 1.1 constant_dynamic-slice_fusion.3
  212.9 1.1 constant_dynamic-slice_fusion.3
  216.8 3.1 convolution_bitcast_fusion.2
  219.9 2.2 fusion.33
  222.1 1.0 copy.55
  223.8 3.6 convolution_bitcast_fusion.5
  227.4 2.2 fusion.35
  229.6 1.6 copy.54
  231.3 105.0 %reduce-scatter.9.cloned.1.call-done = f32[64,256]{1,0:T(8,128)} async-done(((f32[64,2048]{1,0:T(8,128)}), f32[64,256]{1,0:T(8,128)}) %reduce-scatter.9.cloned.1.call-update) | async-done | bytes 65552 | tf_op jit(solution)/shard_map/reduce_scatter | solution.py:109
  336.4 76.9 %reduce-scatter.7.cloned.1.call-done = f32[64,256]{1,0:T(8,128)} async-done(((f32[64,4096]{1,0:T(8,128)}), f32[64,256]{1,0:T(8,128)}) %reduce-scatter.7.cloned.1.call-update) | async-done | bytes 65552 | tf_op jit(solution)/shard_map/reduce_scatter | solution.py:108
  413.3 0.9 add.86
  414.3 66.1 %psum.21 = f32[64,64]{0,1:T(8,128)S(1)} all-reduce(f32[64,64]{0,1:T(8,128)S(1)} %fusion.117), channel_id=1, replica_groups=mesh['row'=8,'col'=16] {'row','col'}, use_global_device_ids=true, to_apply=%region_5.8 | all-reduce | flops 4096 | bytes 32768 | tf_op jit(solution)/shard_map/psum | solution.py:117
  480.6 5.8 cholesky.44
  487.8 4.9 custom-call.6
  493.0 17.4 %all_gather.29 = bf16[64,4096]{1,0:T(8,128)(2,1)S(1)} all-gather(bf16[64,256]{1,0:T(8,128)(2,1)S(1)} %convolution_convert_fusion), channel_id=1, replica_groups=mesh['row'=8,'col'=16] {'col'}, dimensions={1}, use_global_device_ids=true | all-gather | bytes 557056 | tf_op jit(solution)/shard_map/all_gather | solution.py:87
  511.0 3.1 convolution_bitcast_fusion.1
  514.1 2.2 fusion.29
  516.3 1.0 copy.57
  517.4 18.7 %all_gather.28 = bf16[64,2048]{1,0:T(8,128)(2,1)S(1)} all-gather(bf16[64,256]{1,0:T(8,128)(2,1)S(1)} %convolution_convert_fusion), channel_id=1, replica_groups=mesh['row'=8,'col'=16] {'row'}, dimensions={1}, use_global_device_ids=true | all-gather | bytes 294912 | tf_op jit(solution)/shard_map/all_gather | solution.py:90
  536.7 3.6 convolution_bitcast_fusion.4
  540.3 2.2 fusion.31
  542.5 1.6 copy.56
  544.2 5.1 reduce-scatter.13.cloned.1.call-done
  549.3 76.8 %reduce-scatter.11.cloned.1.call-done = f32[64,256]{1,0:T(8,128)} async-done(((f32[64,4096]{1,0:T(8,128)}), f32[64,256]{1,0:T(8,128)}) %reduce-scatter.11.cloned.1.call-update) | async-done | bytes 65552 | tf_op jit(solution)/shard_map/reduce_scatter | solution.py:108
  626.1 0.9 add.88
  627.2 66.2 %psum.22 = f32[64,64]{0,1:T(8,128)S(1)} all-reduce(f32[64,64]{0,1:T(8,128)S(1)} %fusion.118), channel_id=1, replica_groups=mesh['row'=8,'col'=16] {'row','col'}, use_global_device_ids=true, to_apply=%region_10.15 | all-reduce | flops 4096 | bytes 32768 | tf_op jit(solution)/shard_map/psum | solution.py:117
  693.5 5.8 cholesky.55
  700.7 4.9 custom-call.7
  705.6 0.9 fusion.116
  706.5 17.4 %all_gather.31 = bf16[64,4096]{1,0:T(8,128)(2,1)S(1)} all-gather(bf16[64,256]{1,0:T(8,128)(2,1)S(1)} %get-tuple-element.86), channel_id=1, replica_groups=mesh['row'=8,'col'=16] {'col'}, dimensions={1}, use_global_device_ids=true | all-gather | bytes 557056 | tf_op jit(solution)/shard_map/all_gather | solution.py:87
  724.5 3.1 convolution_bitcast_fusion
  727.6 2.2 fusion.25
  729.8 1.0 copy.59
  730.9 18.6 %all_gather.30 = bf16[64,2048]{1,0:T(8,128)(2,1)S(1)} all-gather(bf16[64,256]{1,0:T(8,128)(2,1)S(1)} %get-tuple-element.86), channel_id=1, replica_groups=mesh['row'=8,'col'=16] {'row'}, dimensions={1}, use_global_device_ids=true | all-gather | bytes 294912 | tf_op jit(solution)/shard_map/all_gather | solution.py:90
  750.2 3.6 convolution_bitcast_fusion.3
  753.8 2.2 fusion.27
  756.0 1.6 copy.58
  757.6 5.1 reduce-scatter.17.cloned.1.call-done
  762.7 77.0 %reduce-scatter.15.cloned.1.call-done = f32[64,256]{1,0:T(8,128)} async-done(((f32[64,4096]{1,0:T(8,128)}), f32[64,256]{1,0:T(8,128)}) %reduce-scatter.15.cloned.1.call-update) | async-done | bytes 65552 | tf_op jit(solution)/shard_map/reduce_scatter | solution.py:108
  839.7 1.0 fusion.61
  840.8 66.0 %psum.23 = f32[64,64]{0,1:T(8,128)S(1)} all-reduce(f32[64,64]{0,1:T(8,128)S(1)} %fusion.61), channel_id=1, replica_groups=mesh['row'=8,'col'=16] {'row','col'}, use_global_device_ids=true, to_apply=%region_13.18 | all-reduce | flops 4096 | bytes 32768 | tf_op jit(solution)/shard_map/psum | solution.py:124
  906.8 0.7 copy.43
  (199 shorter events, 68.4 us)
Async XLA Ops:
  7.2 39.2 %copy-start.1 = (s32[1,1,32,2]{2,3,1,0:T(2,128)S(1)}, s32[1,1,32,2]{2,3,1,0:T(2,128)}, u32[]{:S(2)}) copy-start(s32[1,1,32,2]{2,3,1,0:T(2,128)} %param.17) | copy-start | bytes 772
  7.2 39.9 %all-gather.5.cloned.1.call-start = ((), (), s32[]{:S(2)}) async-start(), calls=%async_computation.7 | async-start | bytes 2359296 | tf_op jit(solution)/shard_map/all_gather | solution.py:54
  7.9 90.4 %all-gather.3.cloned.1.call-start = ((), (), s32[]{:S(2)}) async-start(), calls=%async_computation.6 | async-start | bytes 4456448 | tf_op jit(solution)/shard_map/all_gather | solution.py:53
  8.7 327.7 %reduce-scatter.9.cloned.1.call-start = ((), (), s32[]{:S(2)}) async-start(), calls=%async_computation.9 | async-start | bytes 589824 | tf_op jit(solution)/shard_map/reduce_scatter | solution.py:109
  98.4 2.4 copy-start
  223.1 190.1 %reduce-scatter.7.cloned.1.call-start = ((), (), s32[]{:S(2)}) async-start(), calls=%async_computation.8 | async-start | bytes 1114112 | tf_op jit(solution)/shard_map/reduce_scatter | solution.py:108
  231.3 318.0 %reduce-scatter.13.cloned.1.call-start = ((), (), s32[]{:S(2)}) async-start(), calls=%async_computation.11 | async-start | bytes 589824 | tf_op jit(solution)/shard_map/reduce_scatter | solution.py:109
  517.3 108.8 %reduce-scatter.11.cloned.1.call-start = ((), (), s32[]{:S(2)}) async-start(), calls=%async_computation.10 | async-start | bytes 1114112 | tf_op jit(solution)/shard_map/reduce_scatter | solution.py:108
  544.2 218.6 %reduce-scatter.17.cloned.1.call-start = ((), (), s32[]{:S(2)}) async-start(), calls=%async_computation.13 | async-start | bytes 589824 | tf_op jit(solution)/shard_map/reduce_scatter | solution.py:109
  730.8 108.9 %reduce-scatter.15.cloned.1.call-start = ((), (), s32[]{:S(2)}) async-start(), calls=%async_computation.12 | async-start | bytes 1114112 | tf_op jit(solution)/shard_map/reduce_scatter | solution.py:108
Sparse Core Ops, SparseCore 0:
  9.7 30.3 all-gather.4
  42.1 56.1 all-gather.2
  223.2 113.0 reduce-scatter.8
  339.4 73.7 reduce-scatter.6
  517.5 31.7 reduce-scatter.12
  552.3 73.7 reduce-scatter.10
  731.0 31.7 reduce-scatter.16
  765.9 73.7 reduce-scatter.14
where the time goes:
time: 917 us; the launch traced here: 914 us
  waiting for transfers between devices  399 us (44%)
  blocking collectives  307 us (33%)
  local copies, waits for them, and re-layouts  61.1 us (7%)
  matrix products  52.8 us (6%)
  other arithmetic  42.2 us (5%)
  loops' own time  36.9 us (4%)
  between operations  15.1 us (2%)
    reduce_scatter x3, waiting for transfers between devices, network_product(): lax.psum_scatter(row_part, 'col', scatter_dimension=1, tiled=True)  231 us
    psum x2, blocking collectives, local(): gram = lax.psum(local_gram, ('row', 'col')) / cell_total  132 us
    reduce_scatter x3, waiting for transfers between devices, network_product(): lax.psum_scatter(col_part, 'row', scatter_dimension=1, tiled=True)  115 us
    psum x1, blocking collectives, local(): rayleigh = lax.psum(local_form, ('row', 'col')) / cell_total  66 us
    all_gather x3, blocking collectives, project(): lax.all_gather(basis_now, 'col', axis=1, tiled=True)  56.9 us
    all_gather x3, blocking collectives, project(): col_basis = lax.all_gather(basis_now, 'row', axis=1, tiled=True)  52 us
    all_gather x1, waiting for transfers between devices, local(): row_series = lax.all_gather(series, 'col', axis=1, tiled=True)  51.3 us
    another operation x1, loops' own time, local(): lax.fori_loop(0, built_count, build_one, jnp.zeros((slot_total, BLOCK, BL...  36.9 us
  transfers between devices with their start and end apart: 8, of which 7 were waited for; matrix products, arithmetic and copies ran while one was open for 3% of the time, Pallas kernels for 0%

commit v1 on v0

--- a/solution.py
+++ b/solution.py
@@ -9,6 +9,12 @@
 BETA_CORR = 8.0
 GRAM_EPS = 1e-05
 HIGHEST = lax.Precision.HIGHEST
+
+
+def edge_rest(a_name, group_axis, field_in):
+    for no in (a_name, group_axis):
+        field_in = lax.psum(field_in, no)
+    return field_in
 
 
 def lagged_tile(lead_block, trail_block, lag_weight, tile_scale):
@@ -121,7 +127,7 @@
         current = basis.astype(jnp.bfloat16)
     final = network_product(current)
     local_form = jnp.dot(final, current.astype(jnp.float32).T, precision=HIGHEST)
-    rayleigh = lax.psum(local_form, ("row", "col")) / cell_total
+    rayleigh = edge_rest("col", "row", local_form) / cell_total
     return (basis, rayleigh)
 
 

time: 917 us -> 947 us (1.033)
  blocking collectives: 307 us -> 336 us
    psum x1 -> x2, blocking collectives: 66 us -> 94.5 us  [edge_rest(): field_in = lax.psum(field_in, no)]
where the time goes in v1:
time: 947 us; the launch traced here: 943 us
  waiting for transfers between devices  399 us (42%)
  blocking collectives  336 us (35%)
  local copies, waits for them, and re-layouts  61.1 us (6%)
  matrix products  52.8 us (6%)
  other arithmetic  42.2 us (4%)
  loops' own time  36.9 us (4%)
  between operations  15.1 us (2%)
    reduce_scatter x3, waiting for transfers between devices, network_product(): lax.psum_scatter(row_part, 'col', scatter_dimension=1, tiled=True)  231 us
    psum x2, blocking collectives, local(): gram = lax.psum(local_gram, ('row', 'col')) / cell_total  132 us
    reduce_scatter x3, waiting for transfers between devices, network_product(): lax.psum_scatter(col_part, 'row', scatter_dimension=1, tiled=True)  115 us
    psum x2, blocking collectives, edge_rest(): field_in = lax.psum(field_in, no)  94.5 us
    all_gather x3, blocking collectives, project(): lax.all_gather(basis_now, 'col', axis=1, tiled=True)  56.9 us
    all_gather x3, blocking collectives, project(): col_basis = lax.all_gather(basis_now, 'row', axis=1, tiled=True)  52 us
    all_gather x1, waiting for transfers between devices, local(): row_series = lax.all_gather(series, 'col', axis=1, tiled=True)  51.3 us
    another operation x1, loops' own time, local(): lax.fori_loop(0, built_count, build_one, jnp.zeros((slot_total, BLOCK, BL...  36.9 us
  transfers between devices with their start and end apart: 8, of which 7 were waited for; matrix products, arithmetic and copies ran while one was open for 3% of the time, Pallas kernels for 0%

profile of v1, /device:TPU:1, one launch (start us, length us, event | category | flops | bytes accessed | tf_op | source)
XLA Modules:
  0.0 942.8 jit_solution(4889714485644341192)
XLA Ops:
  8.7 14.7 %all_gather.26 = bf16[64,2048]{1,0:T(8,128)(2,1)S(1)} all-gather(bf16[64,256]{1,0:T(8,128)(2,1)} %param.16), channel_id=1, replica_groups=mesh['row'=8,'col'=16] {'row'}, dimensions={1}, use_global_device_ids=true | all-gather | bytes 294912 | tf_op jit(solution)/shard_map/all_gather | solution.py:96
  24.1 22.2 %all_gather.27 = bf16[64,4096]{1,0:T(8,128)(2,1)S(1)} all-gather(bf16[64,256]{1,0:T(8,128)(2,1)} %param.16), channel_id=1, replica_groups=mesh['row'=8,'col'=16] {'col'}, dimensions={1}, use_global_device_ids=true | all-gather | bytes 557056 | tf_op jit(solution)/shard_map/all_gather | solution.py:93
  47.1 51.3 %all-gather.3.cloned.1.call-done = bf16[512,4096]{1,0:T(8,128)(2,1)} async-done(((bf16[512,256]{1,0:T(8,128)(2,1)}), bf16[512,4096]{1,0:T(8,128)(2,1)}) %all-gather.3.cloned.1.call-update) | async-done | bytes 4194320 | tf_op jit(solution)/shard_map/all_gather | solution.py:59
  98.4 2.4 broadcast_in_dim.30
  100.8 116.0 %while.10 = (s32[]{:T(128)}, bf16[32,256,256]{2,1,0:T(8,128)(2,1)}, s32[]{:T(128)}, f32[4]{0:T(128)S(1)}, s32[32]{0:T(128)S(1)}, /*index=5*/bf16[512,4096]{1,0:T...) while((s32[]{:T(128)}, bf16[32,256,256]{2,1,0:T(8,128)(2,1)}, ...), condition=%wide.region_2.3_spmd, body=%wide.region_0.2_spmd.sunk | while | flops 546373632 | bytes 10617143 | solution.py:81
  104.0 1.1 constant_dynamic-slice_fusion.3
  110.4 1.1 constant_dynamic-slice_fusion.3
  116.8 1.1 constant_dynamic-slice_fusion.3
  123.2 1.1 constant_dynamic-slice_fusion.3
  129.6 1.1 constant_dynamic-slice_fusion.3
  136.0 1.1 constant_dynamic-slice_fusion.3
  142.4 1.1 constant_dynamic-slice_fusion.3
  148.8 1.1 constant_dynamic-slice_fusion.3
  155.2 1.1 constant_dynamic-slice_fusion.3
  161.6 1.1 constant_dynamic-slice_fusion.3
  168.0 1.1 constant_dynamic-slice_fusion.3
  174.4 1.1 constant_dynamic-slice_fusion.3
  180.9 1.1 constant_dynamic-slice_fusion.3
  187.3 1.1 constant_dynamic-slice_fusion.3
  193.7 1.1 constant_dynamic-slice_fusion.3
  200.1 1.1 constant_dynamic-slice_fusion.3
  206.5 1.1 constant_dynamic-slice_fusion.3
  212.9 1.1 constant_dynamic-slice_fusion.3
  216.8 3.1 convolution_bitcast_fusion.2
  219.9 2.2 fusion.33
  222.1 1.0 copy.55
  223.8 3.6 convolution_bitcast_fusion.5
  227.4 2.2 fusion.35
  229.6 1.6 copy.54
  231.3 105.0 %reduce-scatter.9.cloned.1.call-done = f32[64,256]{1,0:T(8,128)} async-done(((f32[64,2048]{1,0:T(8,128)}), f32[64,256]{1,0:T(8,128)}) %reduce-scatter.9.cloned.1.call-update) | async-done | bytes 65552 | tf_op jit(solution)/shard_map/reduce_scatter | solution.py:115
  336.4 76.9 %reduce-scatter.7.cloned.1.call-done = f32[64,256]{1,0:T(8,128)} async-done(((f32[64,4096]{1,0:T(8,128)}), f32[64,256]{1,0:T(8,128)}) %reduce-scatter.7.cloned.1.call-update) | async-done | bytes 65552 | tf_op jit(solution)/shard_map/reduce_scatter | solution.py:114
  413.3 0.9 add.88
  414.3 66.1 %psum.28 = f32[64,64]{0,1:T(8,128)S(1)} all-reduce(f32[64,64]{0,1:T(8,128)S(1)} %fusion.117), channel_id=1, replica_groups=mesh['row'=8,'col'=16] {'row','col'}, use_global_device_ids=true, to_apply=%region_5.8 | all-reduce | flops 4096 | bytes 32768 | tf_op jit(solution)/shard_map/psum | solution.py:123
  480.6 5.8 cholesky.44
  487.8 4.9 custom-call.6
  493.0 17.4 %all_gather.29 = bf16[64,4096]{1,0:T(8,128)(2,1)S(1)} all-gather(bf16[64,256]{1,0:T(8,128)(2,1)S(1)} %convolution_convert_fusion), channel_id=1, replica_groups=mesh['row'=8,'col'=16] {'col'}, dimensions={1}, use_global_device_ids=true | all-gather | bytes 557056 | tf_op jit(solution)/shard_map/all_gather | solution.py:93
  511.0 3.1 convolution_bitcast_fusion.1
  514.1 2.2 fusion.29
  516.3 1.0 copy.57
  517.4 18.7 %all_gather.28 = bf16[64,2048]{1,0:T(8,128)(2,1)S(1)} all-gather(bf16[64,256]{1,0:T(8,128)(2,1)S(1)} %convolution_convert_fusion), channel_id=1, replica_groups=mesh['row'=8,'col'=16] {'row'}, dimensions={1}, use_global_device_ids=true | all-gather | bytes 294912 | tf_op jit(solution)/shard_map/all_gather | solution.py:96
  536.7 3.6 convolution_bitcast_fusion.4
  540.3 2.2 fusion.31
  542.5 1.6 copy.56
  544.2 5.1 reduce-scatter.13.cloned.1.call-done
  549.3 76.8 %reduce-scatter.11.cloned.1.call-done = f32[64,256]{1,0:T(8,128)} async-done(((f32[64,4096]{1,0:T(8,128)}), f32[64,256]{1,0:T(8,128)}) %reduce-scatter.11.cloned.1.call-update) | async-done | bytes 65552 | tf_op jit(solution)/shard_map/reduce_scatter | solution.py:114
  626.1 0.9 add.90
  627.2 66.2 %psum.29 = f32[64,64]{0,1:T(8,128)S(1)} all-reduce(f32[64,64]{0,1:T(8,128)S(1)} %fusion.118), channel_id=1, replica_groups=mesh['row'=8,'col'=16] {'row','col'}, use_global_device_ids=true, to_apply=%region_10.15 | all-reduce | flops 4096 | bytes 32768 | tf_op jit(solution)/shard_map/psum | solution.py:123
  693.5 5.8 cholesky.55
  700.7 4.9 custom-call.7
  705.6 0.9 fusion.116
  706.5 17.4 %all_gather.31 = bf16[64,4096]{1,0:T(8,128)(2,1)S(1)} all-gather(bf16[64,256]{1,0:T(8,128)(2,1)S(1)} %get-tuple-element.86), channel_id=1, replica_groups=mesh['row'=8,'col'=16] {'col'}, dimensions={1}, use_global_device_ids=true | all-gather | bytes 557056 | tf_op jit(solution)/shard_map/all_gather | solution.py:93
  724.5 3.1 convolution_bitcast_fusion
  727.6 2.2 fusion.25
  729.8 1.0 copy.59
  730.9 18.6 %all_gather.30 = bf16[64,2048]{1,0:T(8,128)(2,1)S(1)} all-gather(bf16[64,256]{1,0:T(8,128)(2,1)S(1)} %get-tuple-element.86), channel_id=1, replica_groups=mesh['row'=8,'col'=16] {'row'}, dimensions={1}, use_global_device_ids=true | all-gather | bytes 294912 | tf_op jit(solution)/shard_map/all_gather | solution.py:96
  750.2 3.6 convolution_bitcast_fusion.3
  753.8 2.2 fusion.27
  756.0 1.6 copy.58
  757.6 5.1 reduce-scatter.17.cloned.1.call-done
  762.7 77.0 %reduce-scatter.15.cloned.1.call-done = f32[64,256]{1,0:T(8,128)} async-done(((f32[64,4096]{1,0:T(8,128)}), f32[64,256]{1,0:T(8,128)}) %reduce-scatter.15.cloned.1.call-update) | async-done | bytes 65552 | tf_op jit(solution)/shard_map/reduce_scatter | solution.py:114
  839.7 1.0 fusion.61
  840.8 57.9 %psum.30 = f32[64,64]{0,1:T(8,128)S(1)} all-reduce(f32[64,64]{0,1:T(8,128)S(1)} %fusion.61), channel_id=1, replica_groups=mesh['row'=8,'col'=16] {'col'}, use_global_device_ids=true, to_apply=%region_13.18 | all-reduce | flops 4096 | bytes 32768 | tf_op jit(solution)/shard_map/psum | solution.py:16
  898.7 36.6 %psum.31 = f32[64,64]{0,1:T(8,128)S(1)} all-reduce(f32[64,64]{0,1:T(8,128)S(1)} %psum.30), channel_id=1, replica_groups=mesh['row'=8,'col'=16] {'row'}, use_global_device_ids=true, to_apply=%region_14.19 | all-reduce | flops 4096 | bytes 32768 | tf_op jit(solution)/shard_map/psum | solution.py:16
  935.3 0.7 copy.43
  (200 shorter events, 69.1 us)
Async XLA Ops:
  7.2 39.2 %copy-start.1 = (s32[1,1,32,2]{2,3,1,0:T(2,128)S(1)}, s32[1,1,32,2]{2,3,1,0:T(2,128)}, u32[]{:S(2)}) copy-start(s32[1,1,32,2]{2,3,1,0:T(2,128)} %param.17) | copy-start | bytes 772
  7.2 39.9 %all-gather.5.cloned.1.call-start = ((), (), s32[]{:S(2)}) async-start(), calls=%async_computation.7 | async-start | bytes 2359296 | tf_op jit(solution)/shard_map/all_gather | solution.py:60
  7.9 90.4 %all-gather.3.cloned.1.call-start = ((), (), s32[]{:S(2)}) async-start(), calls=%async_computation.6 | async-start | bytes 4456448 | tf_op jit(solution)/shard_map/all_gather | solution.py:59
  8.7 327.7 %reduce-scatter.9.cloned.1.call-start = ((), (), s32[]{:S(2)}) async-start(), calls=%async_computation.9 | async-start | bytes 589824 | tf_op jit(solution)/shard_map/reduce_scatter | solution.py:115
  98.4 2.4 copy-start
  223.1 190.1 %reduce-scatter.7.cloned.1.call-start = ((), (), s32[]{:S(2)}) async-start(), calls=%async_computation.8 | async-start | bytes 1114112 | tf_op jit(solution)/shard_map/reduce_scatter | solution.py:114
  231.3 318.0 %reduce-scatter.13.cloned.1.call-start = ((), (), s32[]{:S(2)}) async-start(), calls=%async_computation.11 | async-start | bytes 589824 | tf_op jit(solution)/shard_map/reduce_scatter | solution.py:115
  517.3 108.8 %reduce-scatter.11.cloned.1.call-start = ((), (), s32[]{:S(2)}) async-start(), calls=%async_computation.10 | async-start | bytes 1114112 | tf_op jit(solution)/shard_map/reduce_scatter | solution.py:114
  544.2 218.6 %reduce-scatter.17.cloned.1.call-start = ((), (), s32[]{:S(2)}) async-start(), calls=%async_computation.13 | async-start | bytes 589824 | tf_op jit(solution)/shard_map/reduce_scatter | solution.py:115
  730.8 108.9 %reduce-scatter.15.cloned.1.call-start = ((), (), s32[]{:S(2)}) async-start(), calls=%async_computation.12 | async-start | bytes 1114112 | tf_op jit(solution)/shard_map/reduce_scatter | solution.py:114
Sparse Core Ops, SparseCore 0:
  9.7 30.3 all-gather.4
  42.1 56.1 all-gather.2
  223.2 113.0 reduce-scatter.8
  339.4 73.7 reduce-scatter.6
  517.5 31.7 reduce-scatter.12
  552.3 73.7 reduce-scatter.10
  731.0 31.7 reduce-scatter.16
  765.9 73.7 reduce-scatter.14
